TPU v7x, 256 devices: a whole 4x4x8 slice. The times are simulated.
256 devices in a mesh: req: 4 (over x), blk: 64 (over z, y, core).
Axes of the slice: x: 4, y: 4, z: 8, core: 2. Of those that a mesh axis runs over, the one named last changes fastest.
Arguments:
- tokens: bfloat16 [4, 8192, 2048], P('req', 'blk'), may hold values from -6 to 6
- block_ids: int32 [4, 128], P('req', 'blk'), may hold values from 0 to 127, as said below
- lengths: int32 [4], P('req'), may hold values from 4097 to 8192, as said below
- page_table: int32 [4, 2, 128], P('req'), may hold values from 0 to 255, as said below
- qkv_weight: bfloat16 [2048, 3072], P(('req', 'blk')), may hold values from -0.125 to 0.125
- q_gain: float32 [256], replicated
- k_gain: float32 [256], replicated
Outputs:
- attended: bfloat16 [4, 8192, 2048], P('req', 'blk')
- kv_cache: bfloat16 [4, 256, 64, 512], P('req', 'blk')
Inputs may be any that keep to these rules, and one draw needn't show every extreme that they name: `lengths`: one prompt has length exactly 8192. `block_ids`: the two entries of one device are b and 127 - b; over a prompt the first entries are a permutation of 0 to 63. `page_table`: each prompt's entries are a permutation of 0 to 255.
All inputs are finite; a program needn't handle non-finite values.
Results may differ from a plain program's by a relative error of at most 0.013.
The roundings to bfloat16 on the way count: a program that leaves them out, or rounds other values in their place, can miss the bound.
Values may be sent and summed in bfloat16 or wider, within the bound.
A program may use at most 128 MiB of HBM per device.

v0:
```python
import math
import jax
import jax.numpy as jnp
from jax import lax
from jax.sharding import PartitionSpec as P

H = 8
KVH = 2
HD = 256
ROPE_BASE = 1000000.0
NORM_EPS = 1e-06
FLOOR_SCORE = -1e30


def head_norm(tensor, scale_gain):
    return (
        tensor
        * lax.rsqrt(jnp.mean(tensor * tensor, axis=-1, keepdims=True) + NORM_EPS)
        * scale_gain
    )


def rotary(tensor, positions):
    half_dim = tensor.shape[-1] // 2
    channel = jnp.arange(half_dim).astype(jnp.float32)
    inverse = jnp.power(jnp.float32(ROPE_BASE), -2.0 * channel / tensor.shape[-1])
    angles = positions.astype(jnp.float32)[:, None] * inverse[None, :]
    cosine = jnp.cos(angles)[:, None, :]
    sine_part = jnp.sin(angles)[:, None, :]
    front_half = tensor[..., :half_dim]
    second = tensor[..., half_dim:]
    return jnp.concatenate(
        [front_half * cosine - second * sine_part, second * cosine + front_half * sine_part], -1
    )


def body(tokens, block_ids, lengths, page_table, qkv_weight, q_gain, k_gain):
    local_rows = tokens[0]
    row_count = local_rows.shape[0]
    blk_rows = row_count // 2
    groups = H // KVH
    projected = jnp.dot(
        local_rows,
        lax.all_gather(qkv_weight, ("req", "blk"), axis=0, tiled=True),
        preferred_element_type=jnp.float32,
    )
    own_ids = block_ids[0]
    positions = (
        own_ids[:, None] * blk_rows + jnp.arange(blk_rows, dtype=jnp.int32)[None, :]
    ).reshape(row_count)
    length = lengths[0]
    query_raw = projected[:, : H * HD].reshape(row_count, H, HD)
    key_raw = projected[:, H * HD : (H + KVH) * HD].reshape(row_count, KVH, HD)
    value_raw = projected[:, (H + KVH) * HD :].reshape(row_count, KVH, HD)
    queries = (
        rotary(head_norm(query_raw, q_gain), positions)
        .astype(jnp.bfloat16)
        .reshape(row_count, KVH, groups, HD)
    )
    send_keys = (
        rotary(head_norm(key_raw, k_gain), positions)
        .astype(jnp.bfloat16)
        .reshape(row_count, KVH * HD)
    )
    send_values = head_norm(value_raw, 1.0).astype(jnp.bfloat16).reshape(row_count, KVH * HD)
    all_ids = lax.all_gather(block_ids, "blk", axis=1, tiled=True)[0]
    table_size = all_ids.shape[0]
    slot_count = page_table.shape[1] * page_table.shape[2] // lax.axis_size("blk")
    my_slots = lax.axis_index("blk") * slot_count + jnp.arange(slot_count, dtype=jnp.int32)
    slot_match = page_table[0][None, :, :] == my_slots[:, None, None]
    head_grid = jnp.arange(page_table.shape[1], dtype=jnp.int32)[None, :, None]
    block_grid = jnp.arange(page_table.shape[2], dtype=jnp.int32)[None, None, :]
    slot_head = jnp.sum(jnp.where(slot_match, head_grid, 0), axis=(1, 2))
    slot_block = jnp.sum(jnp.where(slot_match, block_grid, 0), axis=(1, 2))
    query_live = positions < length
    running_max = jnp.full((row_count, KVH, groups), FLOOR_SCORE, jnp.float32)
    running_sum = jnp.zeros((row_count, KVH, groups), jnp.float32)
    weighted = jnp.zeros((row_count, KVH, groups, HD), jnp.float32)
    pages_out = jnp.zeros((slot_count, blk_rows, 2 * HD), jnp.bfloat16)
    piece_keys = lax.all_gather(send_keys, "blk", axis=0, tiled=True)
    piece_values = lax.all_gather(send_values, "blk", axis=0, tiled=True)
    piece_rows = piece_keys.shape[0]
    global_rows = jnp.arange(piece_rows, dtype=jnp.int32)
    block_index = global_rows // blk_rows
    lookup = jnp.sum(
        jnp.where(
            block_index[:, None] == jnp.arange(table_size, dtype=jnp.int32)[None, :],
            all_ids[None, :],
            0,
        ),
        1,
    )
    key_pos = lookup * blk_rows + global_rows % blk_rows
    key_heads = piece_keys.reshape(piece_rows, KVH, HD)
    value_heads = piece_values.reshape(piece_rows, KVH, HD)
    key_block = math.gcd(piece_rows, 512)

    def one_block(block_number, running):
        block_keys = lax.dynamic_slice_in_dim(key_heads, block_number * key_block, key_block, 0)
        block_values = lax.dynamic_slice_in_dim(value_heads, block_number * key_block, key_block, 0)
        block_pos = lax.dynamic_slice_in_dim(key_pos, block_number * key_block, key_block, 0)
        allowed = (block_pos[None, :] <= positions[:, None]) & (block_pos[None, :] < length)
        old_max, old_sum, old_weighted = running
        scores = jnp.einsum(
            "rgad,kgd->rgak", queries, block_keys, preferred_element_type=jnp.float32
        )
        mask_full = allowed[:, None, None, :]
        new_max = jnp.maximum(old_max, jnp.max(jnp.where(mask_full, scores, FLOOR_SCORE), -1))
        rescale = jnp.exp(old_max - new_max)
        weights = jnp.where(mask_full, jnp.exp(scores - new_max[..., None]), 0.0)
        new_sum = old_sum * rescale + jnp.sum(weights, -1)
        product = jnp.einsum(
            "rgak,kgd->rgad",
            weights.astype(jnp.bfloat16),
            block_values,
            preferred_element_type=jnp.float32,
        )
        return (new_max, new_sum, old_weighted * rescale[..., None] + product)

    running_max, running_sum, weighted = lax.fori_loop(
        0, piece_rows // key_block, one_block, (running_max, running_sum, weighted)
    )
    paired = jnp.concatenate([key_heads, value_heads], -1)
    row_numbers = jnp.arange(piece_rows, dtype=jnp.int32)
    page_offsets = jnp.arange(blk_rows, dtype=jnp.int32)
    page_list = []
    for slot_number in range(slot_count):
        target = slot_block[slot_number] * blk_rows
        is_start = key_pos == target
        present = jnp.any(is_start)
        first_row = jnp.sum(jnp.where(is_start, row_numbers, 0))
        rows_here = lax.dynamic_slice_in_dim(paired, first_row, blk_rows, 0)
        chosen = lax.dynamic_index_in_dim(rows_here, slot_head[slot_number], 1, keepdims=False)
        live_rows = target + page_offsets < length
        chosen = jnp.where(live_rows[:, None], chosen, jnp.zeros_like(chosen))
        page_list.append(jnp.where(present, chosen, pages_out[slot_number]))
    running_max, running_sum, weighted, pages_out = (
        running_max,
        running_sum,
        weighted,
        jnp.stack(page_list),
    )
    divisor = jnp.where(query_live[:, None, None], running_sum, 1.0)
    attended = jnp.where(query_live[:, None, None, None], weighted / divisor[..., None], 0.0)
    attended = attended.reshape(row_count, H * HD).astype(jnp.bfloat16)
    return (attended[None], pages_out[None])


def solution(mesh):
    in_specs = (
        P("req", "blk", None),
        P("req", "blk"),
        P("req"),
        P("req", None, None),
        P(("req", "blk"), None),
        P(),
        P(),
    )
    out_specs = (P("req", "blk", None), P("req", "blk", None, None))
    return jax.shard_map(body, mesh=mesh, in_specs=in_specs, out_specs=out_specs, check_vma=False)
```

profile of v0, /device:TPU:1, one launch (start us, length us, event | category | flops | bytes accessed | tf_op | source)
XLA Modules:
  0.0 402.0 jit_solution(17340536434207153513)
XLA Ops:
  8.0 128.9 %all-gather.4.cloned.1.call-done = bf16[2048,3072]{1,0:T(8,128)(2,1)} async-done(((bf16[8,3072]{1,0:T(8,128)(2,1)}), bf16[2048,3072]{1,0:T(8,128)(2,1)}) %all-gather.4.cloned.1.call-update) | async-done | bytes 12582928 | tf_op jit(solution)/shard_map/all_gather | solution.py:44
  136.8 6.4 %fusion.21 = f32[128,3072]{1,0:T(8,128)S(1)} fusion(bf16[2048,3072]{1,0:T(8,128)(2,1)} %all-gather.4.cloned.1.call-done, bf16[1,128,2048]{2,1,0:T(8,128)(2,1)S(1)} %copy-done), kind=kOutput, calls=%fused_computation.43 | convolution fusion | flops 1610612736 | bytes 14680064 | tf_op jit(solution)/shard_map/dot_general | solution.py:42
  146.1 0.8 copy.65
  157.0 16.9 %all-reduce = s32[128]{0:T(128)S(1)} all-reduce(s32[128]{0:T(128)S(1)} %bitcast_dynamic-update-slice_fusion), channel_id=1, replica_groups=mesh['req'=4,'blk'=64] {'blk'}, use_global_device_ids=true, to_apply=%add | all-reduce | flops 128 | bytes 1024
  173.9 2.5 select_reduce_fusion
  178.8 0.7 fusion.45
  192.6 32.3 %all-gather.8.cloned.1.call-done = bf16[8192,512]{1,0:T(8,128)(2,1)} async-done(((bf16[128,512]{1,0:T(8,128)(2,1)}), bf16[8192,512]{1,0:T(8,128)(2,1)}) %all-gather.8.cloned.1.call-update) | async-done | bytes 8388624 | tf_op jit(solution)/shard_map/all_gather | solution.py:81
  224.9 11.3 %copy.84 = bf16[8192,512]{0,1:T(8,128)(2,1)} copy(bf16[8192,512]{1,0:T(8,128)(2,1)} %all-gather.8.cloned.1.call-done) | data formatting | bytes 16777216
  236.2 74.7 %all-gather.6.cloned.1.call-done = bf16[8192,512]{0,1:T(8,128)(2,1)} async-done(((bf16[128,512]{0,1:T(8,128)(2,1)}), bf16[8192,512]{0,1:T(8,128)(2,1)}) %all-gather.6.cloned.1.call-update) | async-done | bytes 8388624 | tf_op jit(solution)/shard_map/all_gather | solution.py:80
  310.9 1.7 fusion.24
  313.0 77.7 %while.18 = (s32[]{:T(128)}, f32[128,2,4]{0,2,1:T(4,128)S(1)}, f32[128,2,4]{0,2,1:T(4,128)S(1)}, f32[128,2,4,256]{0,3,2,1:T(8,128)S(1)}, s32[8192]{0:T(1024)S(1)...) while((s32[]{:T(128)}, f32[128,2,4]{0,2,1:T(4,128)S(1)}, ...), condition=%wide.region_7.8_spmd.clone, body=%wide.region_4.0_spmd.clone.sunk | while | flops 541988480 | bytes 10298591 | solution.py:120
  313.2 0.7 broadcast_compare_fusion.10
  314.1 1.6 fusion.62
  316.1 1.7 fusion.65
  319.0 1.6 fusion.62
  321.0 1.7 fusion.65
  322.9 0.7 broadcast_compare_fusion.10
  323.9 1.6 fusion.62
  325.9 1.7 fusion.65
  328.7 1.6 fusion.62
  330.7 1.7 fusion.65
  333.6 1.6 fusion.62
  335.6 1.7 fusion.65
  338.4 1.6 fusion.62
  340.4 1.7 fusion.65
  343.3 1.6 fusion.62
  345.3 1.7 fusion.65
  348.2 1.6 fusion.62
  350.2 1.7 fusion.65
  353.0 1.6 fusion.62
  355.0 1.7 fusion.65
  357.9 1.6 fusion.62
  359.9 1.7 fusion.65
  362.7 1.6 fusion.62
  364.7 1.7 fusion.65
  367.6 1.6 fusion.62
  369.6 1.7 fusion.65
  372.4 1.6 fusion.62
  374.5 1.7 fusion.65
  377.3 1.6 fusion.62
  379.3 1.7 fusion.65
  382.2 1.6 fusion.62
  384.2 1.7 fusion.65
  387.0 1.6 fusion.62
  389.0 1.7 fusion.65
  390.9 1.0 copy.83
  393.9 0.8 fusion.27
  394.7 0.7 maximum_bitcast_fusion
  (203 shorter events, 34.8 us)
Async XLA Ops:
  7.2 129.7 %copy-start = (bf16[1,128,2048]{2,1,0:T(8,128)(2,1)S(1)}, bf16[1,128,2048]{2,1,0:T(8,128)(2,1)}, u32[]{:S(2)}) copy-start(bf16[1,128,2048]{2,1,0:T(8,128)(2,1)} %param.9) | copy-start | bytes 1572868
  7.2 129.6 %all-gather.4.cloned.1.call-start = ((), (), s32[]{:S(2)}) async-start(), calls=%async_computation | async-start | bytes 12632064 | tf_op jit(solution)/shard_map/all_gather | solution.py:44
  7.9 136.8 %copy-start.4 = (s32[1,2]{1,0:T(1,128)S(1)}, s32[1,2]{1,0:T(1,128)}, u32[]{:S(2)}) copy-start(s32[1,2]{1,0:T(1,128)} %param.10) | copy-start | bytes 28
  7.9 217.0 %all-gather.8.cloned.1.call-start = ((), (), s32[]{:S(2)}) async-start(), calls=%async_computation.2 | async-start | bytes 8519680 | tf_op jit(solution)/shard_map/all_gather | solution.py:81
  143.2 2.4 copy-start.1
  143.2 3.8 copy-start.3
  143.2 12.3 %copy-start.5 = (u32[256]{0:T(256)S(1)}, u32[256]{0:T(256)}, u32[]{:S(2)}) copy-start(u32[256]{0:T(256)} %constant.200) | copy-start | bytes 3076
  144.6 166.2 %all-gather.6.cloned.1.call-start = ((), (), s32[]{:S(2)}) async-start(), calls=%async_computation.1 | async-start | bytes 8519680 | tf_op jit(solution)/shard_map/all_gather | solution.py:80
  145.4 46.7 %copy-start.2 = (f32[256]{0:T(256)S(1)}, f32[256]{0:T(256)}, u32[]{:S(2)}) copy-start(f32[256]{0:T(256)} %param.14) | copy-start | bytes 3076
Sparse Core Ops, SparseCore 0:
  11.9 124.9 all-gather.3
  144.8 80.1 all-gather.7
  228.2 82.6 all-gather.5
where the time goes:
time: 404 us; the launch traced here: 402 us
  waiting for transfers between devices  237 us (59%)
  matrix products  59.4 us (15%)
  other arithmetic  37.3 us (9%)
  between operations  33 us (8%)
  local copies, waits for them, and re-layouts  17.7 us (4%)
  blocking collectives  16.9 us (4%)
    all_gather x1, waiting for transfers between devices, body(): lax.all_gather(qkv_weight, ('req', 'blk'), axis=0, tiled=True)  129 us
    all_gather x1, waiting for transfers between devices, body(): piece_keys = lax.all_gather(send_keys, 'blk', axis=0, tiled=True)  74.7 us
    all_gather x1, waiting for transfers between devices, body(): piece_values = lax.all_gather(send_values, 'blk', axis=0, tiled=True)  32.3 us
    dot_general x16, matrix products, one_block(): jnp.einsum('rgak,kgd->rgad', weights.astype(jnp.bfloat16), block_values,...  27.5 us
    dot_general x16, matrix products, one_block(): jnp.einsum('rgad,kgd->rgak', queries, block_keys, preferred_element_type=...  25.5 us
    unnamed x1, blocking collectives  16.9 us
    unnamed x18, local copies, waits for them, and re-layouts  12.4 us
    lt x16, other arithmetic, one_block(): block_pos[None, :] < length  11.6 us
  transfers between devices with their start and end apart: 3, of which 3 were waited for; matrix products, arithmetic and copies ran while one was open for 6% of the time, Pallas kernels for 0%

commit v1 on v0

--- a/solution.py
+++ b/solution.py
@@ -77,8 +77,13 @@
     running_sum = jnp.zeros((row_count, KVH, groups), jnp.float32)
     weighted = jnp.zeros((row_count, KVH, groups, HD), jnp.float32)
     pages_out = jnp.zeros((slot_count, blk_rows, 2 * HD), jnp.bfloat16)
-    piece_keys = lax.all_gather(send_keys, "blk", axis=0, tiled=True)
-    piece_values = lax.all_gather(send_values, "blk", axis=0, tiled=True)
+    piece_keys, piece_values = jnp.split(
+        lax.all_gather(
+            jnp.concatenate([send_keys, send_values], axis=1), "blk", axis=0, tiled=True
+        ),
+        [send_keys.shape[1]],
+        axis=1,
+    )
     piece_rows = piece_keys.shape[0]
     global_rows = jnp.arange(piece_rows, dtype=jnp.int32)
     block_index = global_rows // blk_rows

time: 404 us -> 433 us (1.072)
  local copies, waits for them, and re-layouts: 17.7 us -> 85.4 us
  waiting for transfers between devices: 237 us -> 180 us
  matrix products: 59.4 us -> 75.6 us
    all_gather x2 -> x1, waiting for transfers between devices: 107 us -> 51.6 us  [body(): lax.all_gather(jnp.concatenate([send_keys, send_values], axis=1), 'blk',...]
    dynamic_slice x4 -> x32, local copies, waits for them, and re-layouts: 0.39 us -> 34.5 us  [one_block(): lax.dynamic_slice_in_dim(value_heads, block_number * key_block, key_block...]
    reshape x0 -> x2, local copies, waits for them, and re-layouts: none -> 19.7 us  [the longest x1 12.5 us: body(): value_heads = piece_values.reshape(piece_rows, KVH, HD)]
    dot_general x16, matrix products: 27.5 us -> 42.1 us  [one_block(): jnp.einsum('rgak,kgd->rgad', weights.astype(jnp.bfloat16), block_values,...]
    split x0 -> x1, local copies, waits for them, and re-layouts: none -> 11.4 us  [body(): jnp.split(lax.all_gather(jnp.concatenate([send_keys, send_values], axis=1...]
    concatenate x1, local copies, waits for them, and re-layouts: 0.78 us -> 7.37 us  [body(): paired = jnp.concatenate([key_heads, value_heads], -1)]
    unnamed x18 -> x21, local copies, waits for them, and re-layouts: 12.4 us -> 8.42 us
  transfers between devices with their start and end apart: 3 -> 2, of which waited for: 3 -> 2; matrix products, arithmetic and copies ran while one was open for 6% -> 3% of each run, Pallas kernels for 0% -> 0%
where the time goes in v1:
time: 433 us; the launch traced here: 430 us
  waiting for transfers between devices  180 us (42%)
  local copies, waits for them, and re-layouts  85.4 us (20%)
  matrix products  75.6 us (17%)
  other arithmetic  39.2 us (9%)
  between operations  33 us (8%)
  blocking collectives  16.3 us (4%)
    all_gather x1, waiting for transfers between devices, body(): lax.all_gather(qkv_weight, ('req', 'blk'), axis=0, tiled=True)  128 us
    all_gather x1, waiting for transfers between devices, body(): lax.all_gather(jnp.concatenate([send_keys, send_values], axis=1), 'blk',...  51.6 us
    dot_general x16, matrix products, one_block(): jnp.einsum('rgak,kgd->rgad', weights.astype(jnp.bfloat16), block_values,...  42.1 us
    dynamic_slice x32, local copies, waits for them, and re-layouts, one_block(): lax.dynamic_slice_in_dim(value_heads, block_number * key_block, key_block...  34.5 us
    dot_general x16, matrix products, one_block(): jnp.einsum('rgad,kgd->rgak', queries, block_keys, preferred_element_type=...  27.1 us
    unnamed x1, blocking collectives  16.3 us
    reshape x1, local copies, waits for them, and re-layouts, body(): value_heads = piece_values.reshape(piece_rows, KVH, HD)  12.5 us
    lt x16, other arithmetic, one_block(): block_pos[None, :] < length  11.6 us
  transfers between devices with their start and end apart: 2, of which 2 were waited for; matrix products, arithmetic and copies ran while one was open for 3% of the time, Pallas kernels for 0%

profile of v1, /device:TPU:1, one launch (start us, length us, event | category | flops | bytes accessed | tf_op | source)
XLA Modules:
  0.0 430.3 jit_solution(9547353500871212083)
XLA Ops:
  9.2 127.7 %all-gather.3.cloned.1.call-done = bf16[2048,3072]{1,0:T(8,128)(2,1)} async-done(((bf16[8,3072]{1,0:T(8,128)(2,1)}), bf16[2048,3072]{1,0:T(8,128)(2,1)}) %all-gather.3.cloned.1.call-update) | async-done | bytes 12582928 | tf_op jit(solution)/shard_map/all_gather | solution.py:44
  136.8 6.4 %fusion.19 = f32[128,3072]{1,0:T(8,128)S(1)} fusion(bf16[2048,3072]{1,0:T(8,128)(2,1)} %all-gather.3.cloned.1.call-done, bf16[1,128,2048]{2,1,0:T(8,128)(2,1)S(1)} %copy-done), kind=kOutput, calls=%fused_computation.36 | convolution fusion | flops 1610612736 | bytes 14680064 | tf_op jit(solution)/shard_map/dot_general | solution.py:42
  148.6 16.3 %all-reduce = s32[128]{0:T(128)S(1)} all-reduce(s32[128]{0:T(128)S(1)} %bitcast_dynamic-update-slice_fusion.1), channel_id=1, replica_groups=mesh['req'=4,'blk'=64] {'blk'}, use_global_device_ids=true, to_apply=%add | all-reduce | flops 128 | bytes 1024
  164.9 2.5 select_reduce_fusion
  191.2 51.6 %all-gather.5.cloned.1.call-done = bf16[8192,1024]{1,0:T(8,128)(2,1)} async-done(((bf16[128,1024]{1,0:T(8,128)(2,1)}), bf16[8192,1024]{1,0:T(8,128)(2,1)}) %all-gather.5.cloned.1.call-update) | async-done | bytes 16777232 | tf_op jit(solution)/shard_map/all_gather | solution.py:81
  242.8 11.4 %fusion.42 = (bf16[8192,512]{1,0:T(8,128)(2,1)}, bf16[8192,512]{1,0:T(8,128)(2,1)}) fusion(bf16[8192,1024]{1,0:T(8,128)(2,1)} %all-gather.5.cloned.1.call-done), kind=kLoop, calls=%fused_computation.103 | loop fusion | bytes 33554432 | tf_op jit(solution)/shard_map/split | solution.py:80
  254.2 7.1 %copy.72 = bf16[1024,2,8,256]{3,2,0,1:T(8,128)(2,1)} copy(bf16[1024,2,8,256]{3,2,1,0:T(8,128)(2,1)} %bitcast.107) | data formatting | bytes 16777216 | tf_op jit(solution)/shard_map/reshape | solution.py:99
  261.3 7.3 %constant_dynamic-update-slice_fusion = bf16[8192,2,512]{2,0,1:T(8,128)(2,1)} fusion(bf16[1024,2,8,256]{3,2,1,0:T(8,128)(2,1)} %bitcast.108), kind=kLoop, calls=%fused_computation.81 | loop fusion | bytes 16777216
  268.6 12.5 %reshape.385 = bf16[8192,2,256]{2,1,0:T(2,128)(2,1)} reshape(bf16[8192,512]{1,0:T(8,128)(2,1)} %get-tuple-element.301) | data formatting | bytes 16777216 | tf_op jit(solution)/shard_map/reshape | solution.py:100
  281.2 128.2 %while.18 = (s32[]{:T(128)}, f32[128,2,4]{0,2,1:T(4,128)S(1)}, f32[128,2,4]{0,2,1:T(4,128)S(1)}, f32[128,2,4,256]{0,3,2,1:T(8,128)}, s32[8192]{0:T(1024)S(1)}, /...) while((s32[]{:T(128)}, f32[128,2,4]{0,2,1:T(4,128)S(1)}, ...), condition=%wide.region_7.8_spmd.clone, body=%wide.region_4.0_spmd.clone.sunk | while | flops 541988480 | bytes 12395743 | solution.py:125
  282.3 1.7 fusion.58
  284.4 1.4 constant_dynamic-slice_fusion.2
  286.6 1.5 fusion.61
  289.1 1.7 fusion.58
  293.4 2.7 fusion.61
  297.2 1.7 fusion.58
  299.3 1.4 constant_dynamic-slice_fusion.2
  301.5 2.7 fusion.61
  305.3 1.7 fusion.58
  309.6 2.7 fusion.61
  313.4 1.7 fusion.58
  315.5 1.4 constant_dynamic-slice_fusion.2
  317.7 2.7 fusion.61
  321.5 1.7 fusion.58
  325.8 2.7 fusion.61
  329.6 1.7 fusion.58
  331.7 1.4 constant_dynamic-slice_fusion.2
  333.9 2.7 fusion.61
  337.7 1.7 fusion.58
  341.9 2.7 fusion.61
  345.7 1.7 fusion.58
  350.0 2.7 fusion.61
  353.8 1.7 fusion.58
  358.1 2.7 fusion.61
  361.9 1.7 fusion.58
  366.2 2.7 fusion.61
  370.0 1.7 fusion.58
  374.3 2.7 fusion.61
  378.1 1.7 fusion.58
  382.4 2.7 fusion.61
  386.2 1.7 fusion.58
  390.5 2.7 fusion.61
  394.3 1.7 fusion.58
  398.6 2.7 fusion.61
  402.4 1.7 fusion.58
  406.7 2.7 fusion.61
  411.7 7.4 %bitcast_dynamic-update-slice_fusion = bf16[8192,2,512]{2,0,1:T(8,128)(2,1)} fusion(bf16[8192,2,512]{2,0,1:T(8,128)(2,1)} %constant_dynamic-update-slice_fusion, bf16[1024,2,8,256]{3,2,1,0:T(8,128)(2,1)} %bitcast.106), kind=kLoop, calls=%fused_computation.28 | loop fusion | bytes 16777216 | tf_op jit(solution)/shard_map/concatenate | solution.py:128
  419.1 3.6 fusion.24
  (231 shorter events, 67.9 us)
Async XLA Ops:
  7.2 129.7 %copy-start = (bf16[1,128,2048]{2,1,0:T(8,128)(2,1)S(1)}, bf16[1,128,2048]{2,1,0:T(8,128)(2,1)}, u32[]{:S(2)}) copy-start(bf16[1,128,2048]{2,1,0:T(8,128)(2,1)} %param.9) | copy-start | bytes 1572868
  7.2 129.6 %all-gather.3.cloned.1.call-start = ((), (), s32[]{:S(2)}) async-start(), calls=%async_computation | async-start | bytes 12632064 | tf_op jit(solution)/shard_map/all_gather | solution.py:44
  7.9 234.9 %all-gather.5.cloned.1.call-start = ((), (), s32[]{:S(2)}) async-start(), calls=%async_computation.1 | async-start | bytes 17039360 | tf_op jit(solution)/shard_map/all_gather | solution.py:81
  9.1 135.3 %copy-start.2 = (f32[256]{0:T(256)S(1)}, f32[256]{0:T(256)}, u32[]{:S(2)}) copy-start(f32[256]{0:T(256)} %param.15) | copy-start | bytes 3076
  9.1 136.6 %copy-start.4 = (s32[1,2,128]{2,1,0:T(2,128)S(1)}, s32[1,2,128]{2,1,0:T(2,128)}, u32[]{:S(2)}) copy-start(s32[1,2,128]{2,1,0:T(2,128)} %param.12) | copy-start | bytes 3076
  9.1 138.1 %copy-start.6 = (u32[256]{0:T(256)S(1)}, u32[256]{0:T(256)}, u32[]{:S(2)}) copy-start(u32[256]{0:T(256)} %constant.200) | copy-start | bytes 3076
  9.1 139.3 %copy-start.5 = (s32[1,2]{1,0:T(1,128)S(1)}, s32[1,2]{1,0:T(1,128)}, u32[]{:S(2)}) copy-start(s32[1,2]{1,0:T(1,128)} %param.10) | copy-start | bytes 28
  143.2 46.7 %copy-start.3 = (f32[256]{0:T(256)S(1)}, f32[256]{0:T(256)}, u32[]{:S(2)}) copy-start(f32[256]{0:T(256)} %param.14) | copy-start | bytes 3076
  411.7 11.7 %copy-start.1 = (bf16[1,128,2048]{2,1,0:T(8,128)(2,1)S(1)}, bf16[1,128,2048]{2,1,0:T(8,128)(2,1)}, u32[]{:S(2)}) copy-start(bf16[1,128,2048]{2,1,0:T(8,128)(2,1)} %param.9) | copy-start | bytes 1572868
Sparse Core Ops, SparseCore 0:
  11.9 124.9 all-gather.2
  145.8 97.0 all-gather.4
